TPU v7x, 256 devices: a whole 4x4x8 slice. The times are simulated.
256 devices in a mesh: wide: 32 (over z, x), narrow: 8 (over y, core).
Axes of the slice: x: 4, y: 4, z: 8, core: 2. Of those that a mesh axis runs over, the one named last changes fastest.
Arguments:
- hidden_in: bfloat16 [4096, 2048], P(('wide', 'narrow')), may hold values from -6 to 6
- queries: bfloat16 [4096, 2048], P(('wide', 'narrow')), may hold values from -6 to 6
- cache_key: bfloat16 [4096, 128, 256], P(('wide', 'narrow')), may hold values from -6 to 6
- cache_value: bfloat16 [4096, 128, 256], P(('wide', 'narrow')), may hold values from -6 to 6
- new_key: bfloat16 [4096, 256], P(('wide', 'narrow')), may hold values from -6 to 6
- new_value: bfloat16 [4096, 256], P(('wide', 'narrow')), may hold values from -6 to 6
- lengths: int32 [4096], P(('wide', 'narrow')), may hold values from 2 to 128, as said below
- norm_gain: bfloat16 [2048], replicated, may hold values from 0.5 to 1.5
- gate_codes: bfloat16 [256, 2048, 384], P(('wide', 'narrow')), may hold values from -4 to 4
- gate_scale: float32 [256, 16, 3], P(('wide', 'narrow')), may hold values from 0.011048543 to 0.044194173
- up_codes: bfloat16 [256, 2048, 384], P(('wide', 'narrow')), may hold values from -4 to 4
- up_scale: float32 [256, 16, 3], P(('wide', 'narrow')), may hold values from 0.011048543 to 0.044194173
- down_codes: bfloat16 [256, 384, 2048], P(('wide', 'narrow')), may hold values from -4 to 4
- down_scale: float32 [256, 3, 16], P(('wide', 'narrow')), may hold values from 0.018042196 to 0.07216878
- think_ids: int32 [4096, 8], P(('wide', 'narrow')), may hold values from 0 to 127, all different within a row; in each aligned block of 16 rows (0 to 15, 16 to 31, ...) at most 2 rows name the same one
- think_gates: float32 [4096, 8], P(('wide', 'narrow')), may hold values from 0.05 to 0.3
- talker_source: int32 [4096], P(('wide', 'narrow')), may hold values from 0 to 4095, as said below
- talker_gain: bfloat16 [2048], replicated, may hold values from 0.5 to 1.5
- talk_gate_w: bfloat16 [8, 2048, 384], P('narrow'), may hold values from -0.125 to 0.125
- talk_up_w: bfloat16 [8, 2048, 384], P('narrow'), may hold values from -0.125 to 0.125
- talk_down_w: bfloat16 [8, 384, 1024], P('narrow'), may hold values from -0.3125 to 0.3125
- talk_ids: int32 [4096, 2], P(('wide', 'narrow')), may hold values from 0 to 7, all different within a row; in each aligned block of 16 rows (0 to 15, 16 to 31, ...) at most 8 rows name the same one
- talk_gates: float32 [4096, 2], P(('wide', 'narrow')), may hold values from 0.3 to 0.7
Outputs:
- thinker_out: bfloat16 [4096, 2048], P(('wide', 'narrow'))
- talker_out: bfloat16 [4096, 1024], P(('wide', 'narrow'))
Inputs may be any that keep to these rules, and one draw needn't show every extreme that they name: `think_ids`: each row names 8 different thinker experts; among the rows of one device no expert is named by more than 2 rows. `talk_ids`: each position names 2 different talker experts; among the positions of one device no expert is named by more than 8. `lengths`: some row uses all 128 cached positions. `talker_source`: A permutation of the rows. The row feeding a talker position lies on the same narrow index as the position. The rows of one device feed positions on exactly 16 devices, 1 positions on each.
All inputs are finite; a program needn't handle non-finite values.
Results may differ from a plain program's by a relative error of at most 0.018.
Values may be sent and summed in bfloat16 or wider, within the bound.
No kernel may reach another device: no remote copies, remote signals or barrier semaphores. Data moves between devices by JAX's collectives and lax.ppermute only.
A program may use at most 64 MiB of HBM per device.

v0:
```python
import jax
import jax.numpy as jnp
from jax import lax
from jax.sharding import PartitionSpec as P

HEADS = 16
KV_HEADS = 2
HEAD_DIM = 128
BLK = 128
TOP = 8
TTOP = 2
EPSILON = 1e-06


def dequantize(code_block, scale_block):
    height, breadth = code_block.shape
    tiles = code_block.astype(jnp.float32).reshape(height // BLK, BLK, breadth // BLK, BLK)
    tiles = tiles * scale_block[:, None, :, None]
    return tiles.reshape(height, breadth).astype(jnp.bfloat16)


def rms_norm(values, gain):
    values = values.astype(jnp.float32)
    spread = jnp.mean(values * values, axis=-1, keepdims=True)
    return (values * lax.rsqrt(spread + EPSILON) * gain.astype(jnp.float32)).astype(jnp.bfloat16)


def swiglu(inputs, gate_dense, up_dense, down_dense):
    gated = jnp.dot(inputs, gate_dense, preferred_element_type=jnp.float32)
    lifted = jnp.dot(inputs, up_dense, preferred_element_type=jnp.float32)
    middle = (jax.nn.silu(gated) * lifted).astype(jnp.bfloat16)
    return jnp.dot(middle, down_dense, preferred_element_type=jnp.float32).astype(jnp.bfloat16)


def attend(queries, cache_key, cache_value, new_key, new_value, lengths):
    row_count = queries.shape[0]
    positions = cache_key.shape[1]
    groups = HEADS // KV_HEADS
    scaling = HEAD_DIM ** (-0.5)
    asked = queries.reshape(row_count, KV_HEADS, groups, HEAD_DIM)
    cached_keys = cache_key.reshape(row_count, positions, KV_HEADS, HEAD_DIM)
    cached_values = cache_value.reshape(row_count, positions, KV_HEADS, HEAD_DIM)
    scores = (
        jnp.einsum("rkgd,rtkd->rkgt", asked, cached_keys, preferred_element_type=jnp.float32)
        * scaling
    )
    newest_key = new_key.reshape(row_count, KV_HEADS, HEAD_DIM)
    fresh_score = (
        jnp.einsum("rkgd,rkd->rkg", asked, newest_key, preferred_element_type=jnp.float32) * scaling
    )
    places = jnp.arange(positions, dtype=jnp.int32)
    live_mask = places[None, :] < lengths[:, None]
    scores = jnp.where(live_mask[:, None, None, :], scores, -jnp.inf)
    highest = jnp.maximum(jnp.max(scores, axis=-1), fresh_score)
    weights = jnp.exp(scores - highest[..., None])
    own_weight = jnp.exp(fresh_score - highest)
    totals = jnp.sum(weights, axis=-1) + own_weight
    probabilities = (weights / totals[..., None]).astype(jnp.bfloat16)
    own_prob = (own_weight / totals).astype(jnp.bfloat16)
    mixture = jnp.einsum(
        "rkgt,rtkd->rkgd", probabilities, cached_values, preferred_element_type=jnp.float32
    )
    newest = new_value.reshape(row_count, KV_HEADS, 1, HEAD_DIM).astype(jnp.float32)
    mixture = mixture + own_prob.astype(jnp.float32)[..., None] * newest
    return mixture.reshape(row_count, HEADS * HEAD_DIM)


def slot_tables(expert_ids, gate_weights, expert_count, capacity):
    chosen = expert_ids[:, :, None] == jnp.arange(expert_count, dtype=jnp.int32)[None, None, :]
    picked = jnp.any(chosen, axis=1).astype(jnp.int32)
    weight_of = jnp.sum(jnp.where(chosen, gate_weights[:, :, None], jnp.float32(0.0)), axis=1)
    ranks = jnp.cumsum(picked, axis=0) - picked
    onehot = (picked[:, :, None] == 1) & (
        ranks[:, :, None] == jnp.arange(capacity, dtype=jnp.int32)[None, None, :]
    )
    placing = jnp.transpose(onehot, (1, 2, 0))
    return (placing, weight_of)


def local(
    hidden_in,
    queries,
    cache_key,
    cache_value,
    new_key,
    new_value,
    lengths,
    norm_gain,
    gate_codes,
    gate_scale,
    up_codes,
    up_scale,
    down_codes,
    down_scale,
    think_ids,
    think_gates,
    talker_source,
    talker_gain,
    talk_gate_w,
    talk_up_w,
    talk_down_w,
    talk_ids,
    talk_gates,
):
    wide_count = lax.axis_size("wide")
    narrow_count = lax.axis_size("narrow")
    row_count = hidden_in.shape[0]
    breadth = hidden_in.shape[1]
    attended = attend(queries, cache_key, cache_value, new_key, new_value, lengths)
    residual = hidden_in.astype(jnp.float32) + attended
    normed = rms_norm(residual, norm_gain)
    experts = wide_count * narrow_count // 2
    capacity = min(row_count, max(2, 2 * row_count * TOP // experts))
    placing, weight_of = slot_tables(think_ids, think_gates, experts, capacity)
    outgoing = jnp.einsum(
        "ecr,rd->ecd", placing.astype(jnp.bfloat16), normed, preferred_element_type=jnp.float32
    ).astype(jnp.bfloat16)
    doubled = jnp.broadcast_to(outgoing[:, None], (experts, 2, capacity, breadth)).reshape(
        wide_count, narrow_count, capacity, breadth
    )
    arrived = lax.all_to_all(
        lax.all_to_all(doubled, "wide", split_axis=0, concat_axis=0, tiled=True),
        "narrow",
        split_axis=1,
        concat_axis=1,
        tiled=True,
    )
    gate_dense = dequantize(gate_codes[0], gate_scale[0])
    up_dense = dequantize(up_codes[0], up_scale[0])
    down_dense = dequantize(down_codes[0], down_scale[0])
    produced = swiglu(arrived.reshape(-1, breadth), gate_dense, up_dense, down_dense)
    produced = produced.reshape(wide_count, narrow_count, capacity, breadth)
    returned = lax.all_to_all(
        lax.all_to_all(produced, "wide", split_axis=0, concat_axis=0, tiled=True),
        "narrow",
        split_axis=1,
        concat_axis=1,
        tiled=True,
    )
    paired = returned.reshape(experts, 2, capacity, breadth)
    summed = paired[:, 0].astype(jnp.float32) + paired[:, 1].astype(jnp.float32)
    combine = placing.astype(jnp.float32) * jnp.transpose(weight_of)[:, None, :]
    routed = jnp.einsum("ecr,ecd->rd", combine, summed, precision=lax.Precision.HIGHEST)
    thinker_out = (residual + routed).astype(jnp.bfloat16)
    own_wide = talker_source // row_count // narrow_count
    own_local = talker_source % row_count
    gathered = lax.all_gather(thinker_out, "wide", axis=0, tiled=True)
    talker_in = jnp.take(gathered, own_wide * row_count + own_local, axis=0)
    talker_normed = rms_norm(talker_in, talker_gain)
    talk_capacity = min(row_count, max(2, 2 * row_count * TTOP // narrow_count))
    talk_placing, talk_weight = slot_tables(talk_ids, talk_gates, narrow_count, talk_capacity)
    talk_outgoing = jnp.einsum(
        "ecr,rd->ecd",
        talk_placing.astype(jnp.bfloat16),
        talker_normed,
        preferred_element_type=jnp.float32,
    ).astype(jnp.bfloat16)
    incoming = lax.all_to_all(talk_outgoing, "narrow", split_axis=0, concat_axis=0, tiled=True)
    sources = incoming.shape[0]
    items = incoming.shape[1]
    result = swiglu(incoming.reshape(-1, breadth), talk_gate_w[0], talk_up_w[0], talk_down_w[0])
    talk_done = result.reshape(sources, items, -1)
    talk_back = lax.all_to_all(talk_done, "narrow", split_axis=0, concat_axis=0, tiled=True)
    talk_combine = talk_placing.astype(jnp.float32) * jnp.transpose(talk_weight)[:, None, :]
    talked = jnp.einsum(
        "ecr,ecd->rd", talk_combine, talk_back.astype(jnp.float32), precision=lax.Precision.HIGHEST
    )
    return (thinker_out, talked.astype(jnp.bfloat16))


def solution(mesh):
    return jax.shard_map(
        local,
        mesh=mesh,
        in_specs=(
            P(("wide", "narrow"), None),
            P(("wide", "narrow"), None),
            P(("wide", "narrow"), None, None),
            P(("wide", "narrow"), None, None),
            P(("wide", "narrow"), None),
            P(("wide", "narrow"), None),
            P(("wide", "narrow")),
            P(),
            P(("wide", "narrow"), None, None),
            P(("wide", "narrow"), None, None),
            P(("wide", "narrow"), None, None),
            P(("wide", "narrow"), None, None),
            P(("wide", "narrow"), None, None),
            P(("wide", "narrow"), None, None),
            P(("wide", "narrow"), None),
            P(("wide", "narrow"), None),
            P(("wide", "narrow")),
            P(),
            P("narrow", None, None),
            P("narrow", None, None),
            P("narrow", None, None),
            P(("wide", "narrow"), None),
            P(("wide", "narrow"), None),
        ),
        out_specs=(P(("wide", "narrow"), None), P(("wide", "narrow"), None)),
        check_vma=False,
    )
```

profile of v0, /device:TPU:1, one launch (start us, length us, event | category | flops | bytes accessed | tf_op | source)
XLA Modules:
  0.0 348.2 jit_solution(10771011624162334648)
XLA Ops:
  17.8 60.3 %all_to_all.30 = bf16[32,8,2,2048]{3,2,1,0:T(2,128)(2,1)S(1)} all-to-all(bf16[32,8,2,2048]{3,2,1,0:T(2,128)(2,1)S(1)} %bitcast.148), channel_id=1, replica_groups=mesh['wide'=32,'narrow'=8] {'wide'}, dimensions={0} | all-to-all | bytes 4194304 | tf_op jit(solution)/shard_map/all_to_all | solution.py:122
  78.1 3.1 copy.109
  81.2 7.4 %all-to-all-start.1 = ((bf16[32,8,2,2048]{3,2,0,1:T(2,128)(2,1)}), bf16[32,8,2,2048]{3,2,0,1:T(2,128)(2,1)}, u32[]{:S(2)}, u32[]{:S(2)}) async-start(bf16[32,8,2,2048]{3,2,0,1:T(2,128)(2,1)} %copy.109), calls=%async_computation.1 | async-start | bytes 4194304 | tf_op jit(solution)/shard_map/all_to_all | solution.py:121
  90.7 4.3 %copy.130 = f32[48,8,16,128]{3,2,1,0:T(8,128)} copy(f32[48,8,16,128]{3,1,2,0:T(8,128)} %bitcast.146) | data formatting | bytes 6291456
  95.1 2.1 copy.112
  97.2 2.7 copy.132
  101.9 13.0 %all-to-all-done.1 = bf16[32,8,2,2048]{3,2,0,1:T(2,128)(2,1)} async-done(((bf16[32,8,2,2048]{3,2,0,1:T(2,128)(2,1)}), bf16[32,8,2,2048]{3,2,0,1:T(2,128)(2,1)}, u32[]{:S(2)}, u32[]{:S(2)}) %all-to-all-start.1) | async-done | bytes 2097184 | tf_op jit(solution)/shard_map/all_to_all | solution.py:121
  114.9 5.2 %copy.110 = bf16[32,8,2,2048]{3,2,1,0:T(2,128)(2,1)} copy(bf16[32,8,2,2048]{3,2,0,1:T(2,128)(2,1)} %all-to-all-done.1) | data formatting | bytes 4194304 | tf_op jit(solution)/shard_map/all_to_all | solution.py:121
  120.1 4.1 %reshape.190 = bf16[512,2048]{1,0:T(8,128)(2,1)} reshape(bf16[32,8,2,2048]{3,2,1,0:T(2,128)(2,1)} %copy.110) | data formatting | bytes 4194304 | tf_op jit(solution)/shard_map/reshape | solution.py:131
  124.1 4.2 %fusion.8 = f32[512,384]{1,0:T(8,128)} fusion(bf16[512,2048]{1,0:T(8,128)(2,1)} %reshape.190, bf16[48,8,16,128]{3,2,1,0:T(8,128)(2,1)} %bitcast.152), kind=kOutput, calls=%fused_computation.16 | convolution fusion | flops 805306368 | bytes 4456448 | tf_op jit(solution)/shard_map/dot_general | solution.py:29
  130.3 7.1 %convolution_convert_fusion = bf16[512,2048]{1,0:T(8,128)(2,1)} fusion(f32[48,8,16,128]{3,2,1,0:T(8,128)} %bitcast.150, bf16[1,384,2048]{2,1,0:T(8,128)(2,1)} %param.35, bf16[512,2048]{1,0:T(8,128)(2,1)} %reshape.190, bf16[48,8,16,128]{3,2,1,0:T(8,128)(2,1)S(1)} %bitcast.151, f32[512,384]{1,0:T(8,128)} %fusion.8), kind=kOutput, calls=%fused_computation.5 | convolution fusion | flops 1615200256 | bytes 11272192 | tf_op jit(solution)/shard_map/dot_general | solution.py:32
  137.4 4.4 %reshape.191 = bf16[32,8,2,2048]{3,2,1,0:T(2,128)(2,1)} reshape(bf16[512,2048]{1,0:T(8,128)(2,1)} %convolution_convert_fusion) | data formatting | bytes 4194304 | tf_op jit(solution)/shard_map/reshape | solution.py:132
  141.8 53.8 %all_to_all.31 = bf16[32,8,2,2048]{3,2,1,0:T(2,128)(2,1)S(1)} all-to-all(bf16[32,8,2,2048]{3,2,1,0:T(2,128)(2,1)} %reshape.191), channel_id=1, replica_groups=mesh['wide'=32,'narrow'=8] {'wide'}, dimensions={0} | all-to-all | bytes 4194304 | tf_op jit(solution)/shard_map/all_to_all | solution.py:134
  195.6 3.1 copy.113
  198.7 7.3 %all-to-all-start.3 = ((bf16[32,8,2,2048]{3,2,0,1:T(2,128)(2,1)}), bf16[32,8,2,2048]{3,2,0,1:T(2,128)(2,1)}, u32[]{:S(2)}, u32[]{:S(2)}) async-start(bf16[32,8,2,2048]{3,2,0,1:T(2,128)(2,1)} %copy.113), calls=%async_computation.3 | async-start | bytes 4194304 | tf_op jit(solution)/shard_map/all_to_all | solution.py:133
  206.2 26.1 %all-to-all-done.3 = bf16[32,8,2,2048]{3,2,0,1:T(2,128)(2,1)} async-done(((bf16[32,8,2,2048]{3,2,0,1:T(2,128)(2,1)}), bf16[32,8,2,2048]{3,2,0,1:T(2,128)(2,1)}, u32[]{:S(2)}, u32[]{:S(2)}) %all-to-all-start.3) | async-done | bytes 2097184 | tf_op jit(solution)/shard_map/all_to_all | solution.py:133
  232.4 3.8 %copy.114 = bf16[32,8,2,2048]{3,2,1,0:T(2,128)(2,1)S(1)} copy(bf16[32,8,2,2048]{3,2,0,1:T(2,128)(2,1)} %all-to-all-done.3) | data formatting | bytes 4194304 | tf_op jit(solution)/shard_map/all_to_all | solution.py:133
  237.4 2.9 fusion.2
  240.7 68.5 %all-gather.2.cloned.1.call-done = bf16[512,2048]{1,0:T(8,128)(2,1)} async-done(((bf16[16,2048]{1,0:T(8,128)(2,1)}), bf16[512,2048]{1,0:T(8,128)(2,1)}) %all-gather.2.cloned.1.call-update) | async-done | bytes 2097168 | tf_op jit(solution)/shard_map/all_gather | solution.py:147
  309.2 2.5 gather_fusion
  312.2 15.9 %all_to_all.32 = bf16[8,8,2048]{2,1,0:T(8,128)(2,1)S(1)} all-to-all(bf16[8,8,2048]{2,1,0:T(8,128)(2,1)S(1)} %convolution_convert_fusion.2), channel_id=1, replica_groups=mesh['wide'=32,'narrow'=8] {'narrow'}, dimensions={0} | all-to-all | bytes 524288 | tf_op jit(solution)/shard_map/all_to_all | solution.py:158
  328.4 2.5 fusion.22
  330.9 4.3 %all-to-all-start.5 = ((bf16[8,8,1024]{2,1,0:T(8,128)(2,1)}), bf16[8,8,1024]{2,1,0:T(8,128)(2,1)S(1)}, u32[]{:S(2)}, u32[]{:S(2)}) async-start(bf16[8,8,1024]{2,1,0:T(8,128)(2,1)} %fusion.22), calls=%async_computation.5 | async-start | bytes 262144 | tf_op jit(solution)/shard_map/all_to_all | solution.py:163
  335.2 5.3 %all-to-all-done.5 = bf16[8,8,1024]{2,1,0:T(8,128)(2,1)S(1)} async-done(((bf16[8,8,1024]{2,1,0:T(8,128)(2,1)}), bf16[8,8,1024]{2,1,0:T(8,128)(2,1)S(1)}, u32[]{:S(2)}, u32[]{:S(2)}) %all-to-all-start.5) | async-done | bytes 131104 | tf_op jit(solution)/shard_map/all_to_all | solution.py:163
  (84 shorter events, 19.9 us)
Async XLA Ops:
  7.2 321.3 %copy-start = (bf16[1,2048,384]{2,1,0:T(8,128)(2,1)S(1)}, bf16[1,2048,384]{2,1,0:T(8,128)(2,1)}, u32[]{:S(2)}) copy-start(bf16[1,2048,384]{2,1,0:T(8,128)(2,1)} %param.42) | copy-start | bytes 4718596
  9.7 4.7 %copy-start.5 = (bf16[16,2048]{1,0:T(8,128)(2,1)S(1)}, bf16[16,2048]{1,0:T(8,128)(2,1)}, u32[]{:S(2)}) copy-start(bf16[16,2048]{1,0:T(8,128)(2,1)} %param.23) | copy-start | bytes 196612
  9.8 4.8 %copy-start.7 = (s32[16,8]{0,1:T(8,128)S(1)}, s32[16,8]{0,1:T(8,128)}, u32[]{:S(2)}) copy-start(s32[16,8]{0,1:T(8,128)} %param.37) | copy-start | bytes 1540
  11.7 3.1 copy-start.8
  81.2 7.4 %copy-start.2 = (bf16[1,2048,384]{2,1,0:T(8,128)(2,1)S(1)}, bf16[1,2048,384]{2,1,0:T(8,128)(2,1)}, u32[]{:S(2)}) copy-start(bf16[1,2048,384]{2,1,0:T(8,128)(2,1)} %param.31) | copy-start | bytes 4718596
  81.2 33.7 %all-to-all-start.1 = ((bf16[32,8,2,2048]{3,2,0,1:T(2,128)(2,1)}), bf16[32,8,2,2048]{3,2,0,1:T(2,128)(2,1)}, u32[]{:S(2)}, u32[]{:S(2)}) async-start(bf16[32,8,2,2048]{3,2,0,1:T(2,128)(2,1)} %copy.109), calls=%async_computation.1 | async-start | bytes 4194304 | tf_op jit(solution)/shard_map/all_to_all | solution.py:121
  90.7 4.4 %copy-start.12 = (f32[1,16,3]{1,0,2:T(1,128)S(1)}, f32[1,16,3]{1,0,2:T(1,128)}, u32[]{:S(2)}) copy-start(f32[1,16,3]{1,0,2:T(1,128)} %param.32) | copy-start | bytes 580
  90.7 4.4 %copy-start.3 = (bf16[1,2048,384]{2,1,0:T(8,128)(2,1)S(1)}, bf16[1,2048,384]{2,1,0:T(8,128)(2,1)}, u32[]{:S(2)}) copy-start(bf16[1,2048,384]{2,1,0:T(8,128)(2,1)} %param.33) | copy-start | bytes 4718596
  97.2 2.7 copy-start.13
  97.2 2.7 copy-start.14
  97.2 2.9 copy-start.1
  198.7 7.3 %copy-start.9 = (f32[16,8]{0,1:T(8,128)S(1)}, f32[16,8]{0,1:T(8,128)}, u32[]{:S(2)}) copy-start(f32[16,8]{0,1:T(8,128)} %param.38) | copy-start | bytes 1540
  198.7 33.7 %all-to-all-start.3 = ((bf16[32,8,2,2048]{3,2,0,1:T(2,128)(2,1)}), bf16[32,8,2,2048]{3,2,0,1:T(2,128)(2,1)}, u32[]{:S(2)}, u32[]{:S(2)}) async-start(bf16[32,8,2,2048]{3,2,0,1:T(2,128)(2,1)} %copy.113), calls=%async_computation.3 | async-start | bytes 4194304 | tf_op jit(solution)/shard_map/all_to_all | solution.py:133
  206.0 103.2 %all-gather.2.cloned.1.call-start = ((), (), s32[]{:S(2)}) async-start(), calls=%async_computation.6 | async-start | bytes 2162688 | tf_op jit(solution)/shard_map/all_gather | solution.py:147
  236.2 1.2 copy-start.6
  237.3 3.0 copy-start.11
  237.3 3.3 copy-start.10
  237.3 3.3 copy-start.16
  237.4 90.7 %copy-start.4 = (bf16[1,2048,384]{2,1,0:T(8,128)(2,1)S(1)}, bf16[1,2048,384]{2,1,0:T(8,128)(2,1)}, u32[]{:S(2)}) copy-start(bf16[1,2048,384]{2,1,0:T(8,128)(2,1)} %param.41) | copy-start | bytes 4718596
  328.1 7.2 %copy-start.15 = (f32[16,2]{0,1:T(2,128)S(1)}, f32[16,2]{0,1:T(2,128)}, u32[]{:S(2)}) copy-start(f32[16,2]{0,1:T(2,128)} %param.45) | copy-start | bytes 388
  330.9 9.6 %all-to-all-start.5 = ((bf16[8,8,1024]{2,1,0:T(8,128)(2,1)}), bf16[8,8,1024]{2,1,0:T(8,128)(2,1)S(1)}, u32[]{:S(2)}, u32[]{:S(2)}) async-start(bf16[8,8,1024]{2,1,0:T(8,128)(2,1)} %fusion.22), calls=%async_computation.5 | async-start | bytes 262144 | tf_op jit(solution)/shard_map/all_to_all | solution.py:163
Sparse Core Ops, SparseCore 0:
  240.4 68.7 all-gather.1
where the time goes:
time: 349 us; the launch traced here: 348 us
  blocking collectives  130 us (37%)
  waiting for transfers between devices  113 us (32%)
  local copies, waits for them, and re-layouts  44.8 us (13%)
  matrix products  22.4 us (6%)
  starting transfers between devices  19 us (5%)
  between operations  14.3 us (4%)
  other arithmetic  4.66 us (1%)
    all_gather x1, waiting for transfers between devices, local(): gathered = lax.all_gather(thinker_out, 'wide', axis=0, tiled=True)  68.5 us
    all_to_all x1, blocking collectives, local(): lax.all_to_all(doubled, 'wide', split_axis=0, concat_axis=0, tiled=True)  60.3 us
    all_to_all x1, blocking collectives, local(): lax.all_to_all(produced, 'wide', split_axis=0, concat_axis=0, tiled=True)  53.8 us
    all_to_all x1, waiting for transfers between devices, local(): lax.all_to_all(lax.all_to_all(produced, 'wide', split_axis=0, concat_axis...  26.1 us
    all_to_all x1, blocking collectives, local(): lax.all_to_all(talk_outgoing, 'narrow', split_axis=0, concat_axis=0, tile...  15.9 us
    all_to_all x1, waiting for transfers between devices, local(): lax.all_to_all(lax.all_to_all(doubled, 'wide', split_axis=0, concat_axis=...  13 us
    dot_general x2, matrix products, swiglu(): jnp.dot(middle, down_dense, preferred_element_type=jnp.float32)  9.6 us
    unnamed x42, local copies, waits for them, and re-layouts  8.38 us
  transfers between devices with their start and end apart: 4, of which 4 were waited for; matrix products, arithmetic and copies ran while one was open for 4% of the time, Pallas kernels for 0%

commit v1 on v0

--- a/solution.py
+++ b/solution.py
@@ -144,7 +144,9 @@
     thinker_out = (residual + routed).astype(jnp.bfloat16)
     own_wide = talker_source // row_count // narrow_count
     own_local = talker_source % row_count
-    gathered = lax.all_gather(thinker_out, "wide", axis=0, tiled=True)
+    gathered = jnp.concatenate(
+        lax.all_to_all(jnp.stack([thinker_out] * lax.axis_size("wide")), "wide", 0, 0), axis=0
+    )
     talker_in = jnp.take(gathered, own_wide * row_count + own_local, axis=0)
     talker_normed = rms_norm(talker_in, talker_gain)
     talk_capacity = min(row_count, max(2, 2 * row_count * TTOP // narrow_count))

time: 349 us -> 318 us (0.911)
  waiting for transfers between devices: 113 us -> 92.2 us
  between operations: 14.3 us -> 0.9 us
  starting transfers between devices: 19 us -> 24.6 us
  blocking collectives: 130 us -> 126 us
    all_gather x1 -> x0, waiting for transfers between devices: 68.5 us -> none  [local(): gathered = lax.all_gather(thinker_out, 'wide', axis=0, tiled=True)]
    all_to_all x0 -> x1, waiting for transfers between devices: none -> 47.8 us  [local(): lax.all_to_all(jnp.stack([thinker_out] * lax.axis_size('wide')), 'wide',...]
    all_to_all x0 -> x1, starting transfers between devices: none -> 5.58 us  [local(): lax.all_to_all(jnp.stack([thinker_out] * lax.axis_size('wide')), 'wide',...]
    all_to_all x1, blocking collectives: 15.9 us -> 11.7 us  [local(): lax.all_to_all(talk_outgoing, 'narrow', split_axis=0, concat_axis=0, tile...]
where the time goes in v1:
time: 318 us; the launch traced here: 317 us
  blocking collectives  126 us (40%)
  waiting for transfers between devices  92.2 us (29%)
  local copies, waits for them, and re-layouts  47.1 us (15%)
  starting transfers between devices  24.6 us (8%)
  matrix products  21.8 us (7%)
  other arithmetic  4.64 us (1%)
    all_to_all x1, blocking collectives, local(): lax.all_to_all(doubled, 'wide', split_axis=0, concat_axis=0, tiled=True)  60.3 us
    all_to_all x1, blocking collectives, local(): lax.all_to_all(produced, 'wide', split_axis=0, concat_axis=0, tiled=True)  53.8 us
    all_to_all x1, waiting for transfers between devices, local(): lax.all_to_all(jnp.stack([thinker_out] * lax.axis_size('wide')), 'wide',...  47.8 us
    all_to_all x1, waiting for transfers between devices, local(): lax.all_to_all(lax.all_to_all(produced, 'wide', split_axis=0, concat_axis...  26.2 us
    all_to_all x1, waiting for transfers between devices, local(): lax.all_to_all(lax.all_to_all(doubled, 'wide', split_axis=0, concat_axis=...  12.9 us
    all_to_all x1, blocking collectives, local(): lax.all_to_all(talk_outgoing, 'narrow', split_axis=0, concat_axis=0, tile...  11.7 us
    dot_general x2, matrix products, swiglu(): jnp.dot(middle, down_dense, preferred_element_type=jnp.float32)  9.63 us
    unnamed x42, local copies, waits for them, and re-layouts  8.98 us
  transfers between devices with their start and end apart: 4, of which 4 were waited for; matrix products, arithmetic and copies ran while one was open for 4% of the time, Pallas kernels for 0%

profile of v1, /device:TPU:1, one launch (start us, length us, event | category | flops | bytes accessed | tf_op | source)
XLA Modules:
  0.0 317.2 jit_solution(16308003729001815453)
XLA Ops:
  11.2 60.3 %all_to_all.35 = bf16[32,8,2,2048]{3,2,1,0:T(2,128)(2,1)S(1)} all-to-all(bf16[32,8,2,2048]{3,2,1,0:T(2,128)(2,1)S(1)} %bitcast.149), channel_id=1, replica_groups=mesh['wide'=32,'narrow'=8] {'wide'}, dimensions={0} | all-to-all | bytes 4194304 | tf_op jit(solution)/shard_map/all_to_all | solution.py:122
  71.6 3.1 copy.109
  74.6 7.4 %all-to-all-start.1 = ((bf16[32,8,2,2048]{3,2,0,1:T(2,128)(2,1)}), bf16[32,8,2,2048]{3,2,0,1:T(2,128)(2,1)}, u32[]{:S(2)}, u32[]{:S(2)}) async-start(bf16[32,8,2,2048]{3,2,0,1:T(2,128)(2,1)} %copy.109), calls=%async_computation.1 | async-start | bytes 4194304 | tf_op jit(solution)/shard_map/all_to_all | solution.py:121
  84.2 4.3 %copy.130 = f32[48,8,16,128]{3,2,1,0:T(8,128)} copy(f32[48,8,16,128]{3,1,2,0:T(8,128)} %bitcast.147) | data formatting | bytes 6291456
  90.8 2.7 copy.132
  95.4 12.9 %all-to-all-done.1 = bf16[32,8,2,2048]{3,2,0,1:T(2,128)(2,1)} async-done(((bf16[32,8,2,2048]{3,2,0,1:T(2,128)(2,1)}), bf16[32,8,2,2048]{3,2,0,1:T(2,128)(2,1)}, u32[]{:S(2)}, u32[]{:S(2)}) %all-to-all-start.1) | async-done | bytes 2097184 | tf_op jit(solution)/shard_map/all_to_all | solution.py:121
  108.4 5.2 %copy.110 = bf16[32,8,2,2048]{3,2,1,0:T(2,128)(2,1)} copy(bf16[32,8,2,2048]{3,2,0,1:T(2,128)(2,1)} %all-to-all-done.1) | data formatting | bytes 4194304 | tf_op jit(solution)/shard_map/all_to_all | solution.py:121
  113.5 4.1 %reshape.195 = bf16[512,2048]{1,0:T(8,128)(2,1)} reshape(bf16[32,8,2,2048]{3,2,1,0:T(2,128)(2,1)} %copy.110) | data formatting | bytes 4194304 | tf_op jit(solution)/shard_map/reshape | solution.py:131
  117.6 4.2 %fusion.8 = f32[512,384]{1,0:T(8,128)} fusion(bf16[512,2048]{1,0:T(8,128)(2,1)} %reshape.195, bf16[48,8,16,128]{3,2,1,0:T(8,128)(2,1)} %bitcast.153), kind=kOutput, calls=%fused_computation.16 | convolution fusion | flops 805306368 | bytes 4456448 | tf_op jit(solution)/shard_map/dot_general | solution.py:29
  123.8 7.1 %convolution_convert_fusion = bf16[512,2048]{1,0:T(8,128)(2,1)} fusion(f32[48,8,16,128]{3,2,1,0:T(8,128)} %bitcast.151, bf16[1,384,2048]{2,1,0:T(8,128)(2,1)} %param.35, bf16[512,2048]{1,0:T(8,128)(2,1)} %reshape.195, bf16[48,8,16,128]{3,2,1,0:T(8,128)(2,1)S(1)} %bitcast.152, f32[512,384]{1,0:T(8,128)} %fusion.8), kind=kOutput, calls=%fused_computation.5 | convolution fusion | flops 1615200256 | bytes 11272192 | tf_op jit(solution)/shard_map/dot_general | solution.py:32
  131.0 4.4 %reshape.196 = bf16[32,8,2,2048]{3,2,1,0:T(2,128)(2,1)} reshape(bf16[512,2048]{1,0:T(8,128)(2,1)} %convolution_convert_fusion) | data formatting | bytes 4194304 | tf_op jit(solution)/shard_map/reshape | solution.py:132
  135.3 53.8 %all_to_all.36 = bf16[32,8,2,2048]{3,2,1,0:T(2,128)(2,1)S(1)} all-to-all(bf16[32,8,2,2048]{3,2,1,0:T(2,128)(2,1)} %reshape.196), channel_id=1, replica_groups=mesh['wide'=32,'narrow'=8] {'wide'}, dimensions={0} | all-to-all | bytes 4194304 | tf_op jit(solution)/shard_map/all_to_all | solution.py:134
  189.1 3.1 copy.113
  192.2 7.3 %all-to-all-start.3 = ((bf16[32,8,2,2048]{3,2,0,1:T(2,128)(2,1)}), bf16[32,8,2,2048]{3,2,0,1:T(2,128)(2,1)}, u32[]{:S(2)}, u32[]{:S(2)}) async-start(bf16[32,8,2,2048]{3,2,0,1:T(2,128)(2,1)} %copy.113), calls=%async_computation.3 | async-start | bytes 4194304 | tf_op jit(solution)/shard_map/all_to_all | solution.py:133
  199.7 26.2 %all-to-all-done.3 = bf16[32,8,2,2048]{3,2,0,1:T(2,128)(2,1)} async-done(((bf16[32,8,2,2048]{3,2,0,1:T(2,128)(2,1)}), bf16[32,8,2,2048]{3,2,0,1:T(2,128)(2,1)}, u32[]{:S(2)}, u32[]{:S(2)}) %all-to-all-start.3) | async-done | bytes 2097184 | tf_op jit(solution)/shard_map/all_to_all | solution.py:133
  225.9 3.8 %copy.114 = bf16[32,8,2,2048]{3,2,1,0:T(2,128)(2,1)S(1)} copy(bf16[32,8,2,2048]{3,2,0,1:T(2,128)(2,1)} %all-to-all-done.3) | data formatting | bytes 4194304 | tf_op jit(solution)/shard_map/all_to_all | solution.py:133
  230.8 2.2 fusion.2
  235.3 5.6 %all-to-all-start.4 = ((bf16[32,16,2048]{2,1,0:T(8,128)(2,1)}), bf16[32,16,2048]{2,1,0:T(8,128)(2,1)}, u32[]{:S(2)}, u32[]{:S(2)}) async-start(bf16[32,16,2048]{2,1,0:T(8,128)(2,1)} %stack.2), calls=%async_computation.4 | async-start | bytes 4194304 | tf_op jit(solution)/shard_map/all_to_all | solution.py:148
  241.2 47.8 %all-to-all-done.4 = bf16[32,16,2048]{2,1,0:T(8,128)(2,1)} async-done(((bf16[32,16,2048]{2,1,0:T(8,128)(2,1)}), bf16[32,16,2048]{2,1,0:T(8,128)(2,1)}, u32[]{:S(2)}, u32[]{:S(2)}) %all-to-all-start.4) | async-done | bytes 2097184 | tf_op jit(solution)/shard_map/all_to_all | solution.py:148
  289.1 2.5 gather_fusion
  292.1 11.7 %all_to_all.37 = bf16[8,8,2048]{2,1,0:T(8,128)(2,1)S(1)} all-to-all(bf16[8,8,2048]{2,1,0:T(8,128)(2,1)S(1)} %convolution_convert_fusion.2), channel_id=1, replica_groups=mesh['wide'=32,'narrow'=8] {'narrow'}, dimensions={0} | all-to-all | bytes 524288 | tf_op jit(solution)/shard_map/all_to_all | solution.py:160
  304.2 2.5 fusion.22
  306.7 4.3 %all-to-all-start.6 = ((bf16[8,8,1024]{2,1,0:T(8,128)(2,1)}), bf16[8,8,1024]{2,1,0:T(8,128)(2,1)S(1)}, u32[]{:S(2)}, u32[]{:S(2)}) async-start(bf16[8,8,1024]{2,1,0:T(8,128)(2,1)} %fusion.22), calls=%async_computation.6 | async-start | bytes 262144 | tf_op jit(solution)/shard_map/all_to_all | solution.py:165
  311.0 5.3 %all-to-all-done.6 = bf16[8,8,1024]{2,1,0:T(8,128)(2,1)S(1)} async-done(((bf16[8,8,1024]{2,1,0:T(8,128)(2,1)}), bf16[8,8,1024]{2,1,0:T(8,128)(2,1)S(1)}, u32[]{:S(2)}, u32[]{:S(2)}) %all-to-all-start.6) | async-done | bytes 131104 | tf_op jit(solution)/shard_map/all_to_all | solution.py:165
  (84 shorter events, 24.3 us)
Async XLA Ops:
  0.6 303.6 %copy-start = (bf16[1,2048,384]{2,1,0:T(8,128)(2,1)S(1)}, bf16[1,2048,384]{2,1,0:T(8,128)(2,1)}, u32[]{:S(2)}) copy-start(bf16[1,2048,384]{2,1,0:T(8,128)(2,1)} %param.42) | copy-start | bytes 4718596
  3.2 4.7 %copy-start.5 = (bf16[16,2048]{1,0:T(8,128)(2,1)S(1)}, bf16[16,2048]{1,0:T(8,128)(2,1)}, u32[]{:S(2)}) copy-start(bf16[16,2048]{1,0:T(8,128)(2,1)} %param.23) | copy-start | bytes 196612
  3.2 4.8 %copy-start.7 = (s32[16,8]{0,1:T(8,128)S(1)}, s32[16,8]{0,1:T(8,128)}, u32[]{:S(2)}) copy-start(s32[16,8]{0,1:T(8,128)} %param.37) | copy-start | bytes 1540
  5.2 3.1 copy-start.8
  74.6 7.4 %copy-start.2 = (bf16[1,2048,384]{2,1,0:T(8,128)(2,1)S(1)}, bf16[1,2048,384]{2,1,0:T(8,128)(2,1)}, u32[]{:S(2)}) copy-start(bf16[1,2048,384]{2,1,0:T(8,128)(2,1)} %param.31) | copy-start | bytes 4718596
  74.6 33.7 %all-to-all-start.1 = ((bf16[32,8,2,2048]{3,2,0,1:T(2,128)(2,1)}), bf16[32,8,2,2048]{3,2,0,1:T(2,128)(2,1)}, u32[]{:S(2)}, u32[]{:S(2)}) async-start(bf16[32,8,2,2048]{3,2,0,1:T(2,128)(2,1)} %copy.109), calls=%async_computation.1 | async-start | bytes 4194304 | tf_op jit(solution)/shard_map/all_to_all | solution.py:121
  84.2 4.3 %copy-start.12 = (f32[1,16,3]{1,0,2:T(1,128)S(1)}, f32[1,16,3]{1,0,2:T(1,128)}, u32[]{:S(2)}) copy-start(f32[1,16,3]{1,0,2:T(1,128)} %param.32) | copy-start | bytes 580
  84.2 4.3 %copy-start.3 = (bf16[1,2048,384]{2,1,0:T(8,128)(2,1)S(1)}, bf16[1,2048,384]{2,1,0:T(8,128)(2,1)}, u32[]{:S(2)}) copy-start(bf16[1,2048,384]{2,1,0:T(8,128)(2,1)} %param.33) | copy-start | bytes 4718596
  90.8 2.7 copy-start.13
  90.8 2.7 copy-start.14
  90.8 2.9 copy-start.1
  192.2 7.3 %copy-start.9 = (f32[16,8]{0,1:T(8,128)S(1)}, f32[16,8]{0,1:T(8,128)}, u32[]{:S(2)}) copy-start(f32[16,8]{0,1:T(8,128)} %param.38) | copy-start | bytes 1540
  192.2 33.7 %all-to-all-start.3 = ((bf16[32,8,2,2048]{3,2,0,1:T(2,128)(2,1)}), bf16[32,8,2,2048]{3,2,0,1:T(2,128)(2,1)}, u32[]{:S(2)}, u32[]{:S(2)}) async-start(bf16[32,8,2,2048]{3,2,0,1:T(2,128)(2,1)} %copy.113), calls=%async_computation.3 | async-start | bytes 4194304 | tf_op jit(solution)/shard_map/all_to_all | solution.py:133
  233.1 0.6 copy-start.6
  235.3 5.6 %copy-start.11 = (s32[16,2]{0,1:T(2,128)S(1)}, s32[16,2]{0,1:T(2,128)}, u32[]{:S(2)}) copy-start(s32[16,2]{0,1:T(2,128)} %param.44) | copy-start | bytes 388
  235.3 5.9 %copy-start.10 = (bf16[2048]{0:T(1024)(128)(2,1)S(1)}, bf16[2048]{0:T(1024)(128)(2,1)}, u32[]{:S(2)}) copy-start(bf16[2048]{0:T(1024)(128)(2,1)} %param.40) | copy-start | bytes 12292
  235.3 5.9 %copy-start.16 = (s32[16]{0:T(128)S(1)}, s32[16]{0:T(128)}, u32[]{:S(2)}) copy-start(s32[16]{0:T(128)} %param.39) | copy-start | bytes 196
  235.3 68.6 %copy-start.4 = (bf16[1,2048,384]{2,1,0:T(8,128)(2,1)S(1)}, bf16[1,2048,384]{2,1,0:T(8,128)(2,1)}, u32[]{:S(2)}) copy-start(bf16[1,2048,384]{2,1,0:T(8,128)(2,1)} %param.41) | copy-start | bytes 4718596
  235.3 53.8 %all-to-all-start.4 = ((bf16[32,16,2048]{2,1,0:T(8,128)(2,1)}), bf16[32,16,2048]{2,1,0:T(8,128)(2,1)}, u32[]{:S(2)}, u32[]{:S(2)}) async-start(bf16[32,16,2048]{2,1,0:T(8,128)(2,1)} %stack.2), calls=%async_computation.4 | async-start | bytes 4194304 | tf_op jit(solution)/shard_map/all_to_all | solution.py:148
  303.8 7.2 %copy-start.15 = (f32[16,2]{0,1:T(2,128)S(1)}, f32[16,2]{0,1:T(2,128)}, u32[]{:S(2)}) copy-start(f32[16,2]{0,1:T(2,128)} %param.45) | copy-start | bytes 388
  306.7 9.6 %all-to-all-start.6 = ((bf16[8,8,1024]{2,1,0:T(8,128)(2,1)}), bf16[8,8,1024]{2,1,0:T(8,128)(2,1)S(1)}, u32[]{:S(2)}, u32[]{:S(2)}) async-start(bf16[8,8,1024]{2,1,0:T(8,128)(2,1)} %fusion.22), calls=%async_computation.6 | async-start | bytes 262144 | tf_op jit(solution)/shard_map/all_to_all | solution.py:165
